TPU v7x, 32 devices: a whole 2x2x4 slice. The times are simulated.
32 devices in a mesh: space: 8 (over z, y), halo: 4 (over x, core).
Axes of the slice: x: 2, y: 2, z: 4, core: 2. Of those that a mesh axis runs over, the one named last changes fastest.
Arguments:
- positions: float32 [3, 131072], P(None, 'space'), may hold values from -1 to 1
- masses: float32 [131072], P('space'), may hold values from 0.1 to 10
- centres: float32 [4, 3, 128], P('halo'), may hold values from -0.5 to 0.5
- pair_halo: int32 [4, 2048], P('halo', 'space'), may hold values from 0 to 127
- pair_tile: int32 [4, 2048], P('halo', 'space'), may hold values from 0 to 31
- halo_slot: int32 [4, 128], P('halo'), may hold values from 0 to 127, each once within a row
- feedback: float32 [4, 128], P('halo', 'space'), may hold values from 0.5 to 1.5
- mixing: float32 [3, 128, 128], replicated, may hold values from -0.5 to 0.5
- drive: float32 [3, 128], replicated, may hold values from 0.2 to 1
- readout: float32 [3, 128], replicated, may hold values from -1.5 to 1.5
Outputs:
- displacement: float32 [3, 131072], P(None, 'space')
All inputs are finite; a program needn't handle non-finite values.
Results may differ from a plain program's by a relative error of at most 0.0003.
Values sent between devices are 32-bit elements; how exact they have to be, the bound alone decides.
No kernel may reach another device: no remote copies, remote signals or barrier semaphores. Data moves between devices by JAX's collectives and lax.ppermute only.
A program may use at most 64 MiB of HBM per device.

v0:
```python
import jax
import jax.numpy as jnp
from jax import lax
from jax.sharding import PartitionSpec as P

BLK = 512
ITERS = 8


def spline_basis(offset, knots):
    radial_distance = jnp.sqrt(jnp.sum(offset * offset, axis=0))
    scaled = radial_distance * ((knots - 1) / 2.6)
    knot_index = jnp.arange(knots, dtype=jnp.float32)
    return jnp.maximum(0.0, 1.0 - jnp.abs(scaled[..., None] - knot_index))


def relax(level, phi, mixing, drive, readout):
    state = jnp.zeros((3,) + level.shape, jnp.float32)
    for relax_iteration in range(ITERS):
        average = jnp.mean(state, axis=0)
        fresh = []
        for comp in range(3):
            mixed = jnp.dot(state[comp], mixing[comp], precision=lax.Precision.HIGHEST)
            fresh.append(jnp.tanh(drive[comp] * level + phi[:, None] * mixed + 0.5 * average))
        state = jnp.stack(fresh)
    return jnp.sum(state * readout[:, None, :], axis=0)


def per_device(
    positions, masses, centres, pair_halo, pair_tile, halo_slot, feedback, mixing, drive, readout
):
    knots = mixing.shape[1]
    tile_count = masses.shape[0] // BLK
    number_of_pairs = pair_halo.shape[1]
    places = positions.reshape(3, tile_count, BLK)
    weights = masses.reshape(tile_count, BLK)
    halo_ids = pair_halo[0]
    tile_ids = pair_tile[0]
    centre_rows = centres[0]
    slot_ids = halo_slot[0][halo_ids]
    block = min(64, number_of_pairs // 8)
    offsets = places[:, tile_ids, :] - centre_rows[:, halo_ids][:, :, None]
    offset_blocks = jnp.transpose(offsets.reshape(3, -1, block, BLK), (1, 0, 2, 3))
    weight_blocks = weights[tile_ids].reshape(-1, block, BLK)

    def project(inputs):
        offset_part, weight_part = inputs
        basis = spline_basis(offset_part, knots)
        return jnp.sum(weight_part[:, :, None] * basis, axis=1)

    pair_rows = lax.map(project, (offset_blocks, weight_blocks)).reshape(number_of_pairs, knots)
    slot_total = halo_slot.shape[1]
    wanted = jnp.arange(slot_total, dtype=jnp.int32)
    halo_selection = (slot_ids[None, :] == wanted[:, None]).astype(jnp.float32)
    dense = lax.psum(jnp.dot(halo_selection, pair_rows, precision=lax.Precision.HIGHEST), "space")
    all_feedback = lax.all_gather(feedback[0], "space", axis=0, tiled=True)
    coef_table = relax(jnp.log1p(dense), all_feedback, mixing, drive, readout)
    coef_rows = coef_table[slot_ids].reshape(-1, block, knots)

    def evaluate(inputs):
        offset_part, coef_part = inputs
        basis = spline_basis(offset_part, knots)
        scalar = jnp.sum(basis * coef_part[:, None, :], axis=2)
        return offset_part * scalar[None]

    shifted_positions = lax.map(evaluate, (offset_blocks, coef_rows))
    shifted_positions = jnp.transpose(shifted_positions, (1, 0, 2, 3)).reshape(
        3, number_of_pairs, BLK
    )
    current_tile = jnp.arange(tile_count, dtype=jnp.int32)
    halo_selection = (current_tile[:, None] == tile_ids[None, :]).astype(jnp.float32)
    partial_halo_sum = jnp.einsum(
        "dq,vqn->vdn", halo_selection, shifted_positions, precision=lax.Precision.HIGHEST
    )
    partial_halo_sum = partial_halo_sum.reshape(3, tile_count * BLK)
    return lax.psum(partial_halo_sum, "halo")


def solution(mesh):
    return jax.shard_map(
        per_device,
        mesh=mesh,
        in_specs=(
            P(None, "space"),
            P("space"),
            P("halo", None, None),
            P("halo", "space"),
            P("halo", "space"),
            P("halo", None),
            P("halo", "space"),
            P(),
            P(),
            P(),
        ),
        out_specs=P(None, "space"),
        check_vma=False,
    )
```

profile of v0, /device:TPU:0, one launch (start us, length us, event | category | flops | bytes accessed | tf_op | source)
XLA Modules:
  0.0 229.1 jit_solution(4436138836586837490)
XLA Ops:
  7.5 1.9 gather_fusion
  15.5 40.7 %while.20 = (s32[]{:T(128)}, f32[8,32,128]{2,1,0:T(8,128)S(1)}, f32[8,32,512]{2,1,0:T(8,128)S(1)}, f32[8,3,32,512]{3,2,1,0:T(8,128)S(1)}, s32[]{:T(128)}) while((s32[]{:T(128)}, f32[8,32,128]{2,1,0:T(8,128)S(1)}, f32[8,32,512]{2,1,0:T(8,128)S(1)}, f32[8,3,32,512]{3,2,1,0:T(8,128)S(1)}, s32[]{:T(128)}) %tuple.50), condition=%wide.region_3.4_spmd, body=%wide.region_0.3_spmd.sunk | while | flops 12677122 | bytes 704585 | solution.py:51
  15.6 5.0 %multiply_reduce_fusion.9 = f32[32,128]{1,0:T(8,128)S(1)} fusion(f32[32,512]{1,0:T(8,128)S(1)} %sqrt_multiply_fusion.4, f32[32,512]{1,0:T(8,128)S(1)} %dynamic-slice_bitcast_fusion.4), kind=kLoop, calls=%fused_computation.5.clone.1 | loop fusion | flops 12578816 | bytes 147456 | tf_op jit(solution)/shard_map/while/body/eval_jaxpr/reduce_sum | solution.py:49
  20.7 5.0 %multiply_reduce_fusion.9 = f32[32,128]{1,0:T(8,128)S(1)} fusion(f32[32,512]{1,0:T(8,128)S(1)} %sqrt_multiply_fusion.4, f32[32,512]{1,0:T(8,128)S(1)} %dynamic-slice_bitcast_fusion.4), kind=kLoop, calls=%fused_computation.5.clone.1 | loop fusion | flops 12578816 | bytes 147456 | tf_op jit(solution)/shard_map/while/body/eval_jaxpr/reduce_sum | solution.py:49
  25.8 5.0 %multiply_reduce_fusion.9 = f32[32,128]{1,0:T(8,128)S(1)} fusion(f32[32,512]{1,0:T(8,128)S(1)} %sqrt_multiply_fusion.4, f32[32,512]{1,0:T(8,128)S(1)} %dynamic-slice_bitcast_fusion.4), kind=kLoop, calls=%fused_computation.5.clone.1 | loop fusion | flops 12578816 | bytes 147456 | tf_op jit(solution)/shard_map/while/body/eval_jaxpr/reduce_sum | solution.py:49
  30.9 5.0 %multiply_reduce_fusion.9 = f32[32,128]{1,0:T(8,128)S(1)} fusion(f32[32,512]{1,0:T(8,128)S(1)} %sqrt_multiply_fusion.4, f32[32,512]{1,0:T(8,128)S(1)} %dynamic-slice_bitcast_fusion.4), kind=kLoop, calls=%fused_computation.5.clone.1 | loop fusion | flops 12578816 | bytes 147456 | tf_op jit(solution)/shard_map/while/body/eval_jaxpr/reduce_sum | solution.py:49
  35.9 5.0 %multiply_reduce_fusion.9 = f32[32,128]{1,0:T(8,128)S(1)} fusion(f32[32,512]{1,0:T(8,128)S(1)} %sqrt_multiply_fusion.4, f32[32,512]{1,0:T(8,128)S(1)} %dynamic-slice_bitcast_fusion.4), kind=kLoop, calls=%fused_computation.5.clone.1 | loop fusion | flops 12578816 | bytes 147456 | tf_op jit(solution)/shard_map/while/body/eval_jaxpr/reduce_sum | solution.py:49
  41.0 5.0 %multiply_reduce_fusion.9 = f32[32,128]{1,0:T(8,128)S(1)} fusion(f32[32,512]{1,0:T(8,128)S(1)} %sqrt_multiply_fusion.4, f32[32,512]{1,0:T(8,128)S(1)} %dynamic-slice_bitcast_fusion.4), kind=kLoop, calls=%fused_computation.5.clone.1 | loop fusion | flops 12578816 | bytes 147456 | tf_op jit(solution)/shard_map/while/body/eval_jaxpr/reduce_sum | solution.py:49
  46.1 5.0 %multiply_reduce_fusion.9 = f32[32,128]{1,0:T(8,128)S(1)} fusion(f32[32,512]{1,0:T(8,128)S(1)} %sqrt_multiply_fusion.4, f32[32,512]{1,0:T(8,128)S(1)} %dynamic-slice_bitcast_fusion.4), kind=kLoop, calls=%fused_computation.5.clone.1 | loop fusion | flops 12578816 | bytes 147456 | tf_op jit(solution)/shard_map/while/body/eval_jaxpr/reduce_sum | solution.py:49
  51.2 5.0 %multiply_reduce_fusion.9 = f32[32,128]{1,0:T(8,128)S(1)} fusion(f32[32,512]{1,0:T(8,128)S(1)} %sqrt_multiply_fusion.4, f32[32,512]{1,0:T(8,128)S(1)} %dynamic-slice_bitcast_fusion.4), kind=kLoop, calls=%fused_computation.5.clone.1 | loop fusion | flops 12578816 | bytes 147456 | tf_op jit(solution)/shard_map/while/body/eval_jaxpr/reduce_sum | solution.py:49
  56.2 1.9 gather_fusion.2
  60.6 23.1 %all-reduce = f32[128]{0:T(128)S(1)} all-reduce(f32[128]{0:T(128)S(1)} %bitcast_dynamic-update-slice_fusion.2), channel_id=2, replica_groups=mesh['space'=8,'halo'=4] {'space'}, use_global_device_ids=true, to_apply=%add | all-reduce | flops 128 | bytes 1024
  83.8 47.3 %all-reduce.4.cloned.1.call-done = f32[128,128]{1,0:T(8,128)} async-done(((f32[128,128]{1,0:T(8,128)}), f32[128,128]{1,0:T(8,128)}) %all-reduce.4.cloned.1.call-update) | async-done | bytes 65552 | tf_op jit(solution)/shard_map/psum | solution.py:55
  141.2 44.0 %while.21 = (s32[]{:T(128)}, f32[8,3,32,512]{3,2,0,1:T(8,128)}, f32[8,3,32,512]{3,2,1,0:T(8,128)S(1)}, f32[8,32,128]{2,1,0:T(8,128)S(1)}, s32[]{:T(128)}) while((s32[]{:T(128)}, f32[8,3,32,512]{3,2,0,1:T(8,128)}, f32[8,3,32,512]{3,2,1,0:T(8,128)S(1)}, f32[8,32,128]{2,1,0:T(8,128)S(1)}, s32[]{:T(128)}) %tuple.51), condition=%wide.region_12.13_spmd, body=%wide.region_9.12_spmd.sunk | while | flops 12713986 | bytes 1032773 | solution.py:66
  141.3 4.7 %multiply_reduce_fusion.11 = f32[32,512]{1,0:T(8,128)S(1)} fusion(f32[32,128]{1,0:T(8,128)S(1)} %dynamic-slice_bitcast_fusion.5, f32[32,512]{1,0:T(8,128)S(1)} %sqrt_multiply_fusion.5), kind=kLoop, calls=%fused_computation.10.clone.1 | loop fusion | flops 12566528 | bytes 147456 | tf_op jit(solution)/shard_map/while/body/eval_jaxpr/reduce_sum | solution.py:63
  146.8 4.7 %multiply_reduce_fusion.11 = f32[32,512]{1,0:T(8,128)S(1)} fusion(f32[32,128]{1,0:T(8,128)S(1)} %dynamic-slice_bitcast_fusion.5, f32[32,512]{1,0:T(8,128)S(1)} %sqrt_multiply_fusion.5), kind=kLoop, calls=%fused_computation.10.clone.1 | loop fusion | flops 12566528 | bytes 147456 | tf_op jit(solution)/shard_map/while/body/eval_jaxpr/reduce_sum | solution.py:63
  152.3 4.7 %multiply_reduce_fusion.11 = f32[32,512]{1,0:T(8,128)S(1)} fusion(f32[32,128]{1,0:T(8,128)S(1)} %dynamic-slice_bitcast_fusion.5, f32[32,512]{1,0:T(8,128)S(1)} %sqrt_multiply_fusion.5), kind=kLoop, calls=%fused_computation.10.clone.1 | loop fusion | flops 12566528 | bytes 147456 | tf_op jit(solution)/shard_map/while/body/eval_jaxpr/reduce_sum | solution.py:63
  157.8 4.7 %multiply_reduce_fusion.11 = f32[32,512]{1,0:T(8,128)S(1)} fusion(f32[32,128]{1,0:T(8,128)S(1)} %dynamic-slice_bitcast_fusion.5, f32[32,512]{1,0:T(8,128)S(1)} %sqrt_multiply_fusion.5), kind=kLoop, calls=%fused_computation.10.clone.1 | loop fusion | flops 12566528 | bytes 147456 | tf_op jit(solution)/shard_map/while/body/eval_jaxpr/reduce_sum | solution.py:63
  163.3 4.7 %multiply_reduce_fusion.11 = f32[32,512]{1,0:T(8,128)S(1)} fusion(f32[32,128]{1,0:T(8,128)S(1)} %dynamic-slice_bitcast_fusion.5, f32[32,512]{1,0:T(8,128)S(1)} %sqrt_multiply_fusion.5), kind=kLoop, calls=%fused_computation.10.clone.1 | loop fusion | flops 12566528 | bytes 147456 | tf_op jit(solution)/shard_map/while/body/eval_jaxpr/reduce_sum | solution.py:63
  168.8 4.7 %multiply_reduce_fusion.11 = f32[32,512]{1,0:T(8,128)S(1)} fusion(f32[32,128]{1,0:T(8,128)S(1)} %dynamic-slice_bitcast_fusion.5, f32[32,512]{1,0:T(8,128)S(1)} %sqrt_multiply_fusion.5), kind=kLoop, calls=%fused_computation.10.clone.1 | loop fusion | flops 12566528 | bytes 147456 | tf_op jit(solution)/shard_map/while/body/eval_jaxpr/reduce_sum | solution.py:63
  174.3 4.7 %multiply_reduce_fusion.11 = f32[32,512]{1,0:T(8,128)S(1)} fusion(f32[32,128]{1,0:T(8,128)S(1)} %dynamic-slice_bitcast_fusion.5, f32[32,512]{1,0:T(8,128)S(1)} %sqrt_multiply_fusion.5), kind=kLoop, calls=%fused_computation.10.clone.1 | loop fusion | flops 12566528 | bytes 147456 | tf_op jit(solution)/shard_map/while/body/eval_jaxpr/reduce_sum | solution.py:63
  179.8 4.7 %multiply_reduce_fusion.11 = f32[32,512]{1,0:T(8,128)S(1)} fusion(f32[32,128]{1,0:T(8,128)S(1)} %dynamic-slice_bitcast_fusion.5, f32[32,512]{1,0:T(8,128)S(1)} %sqrt_multiply_fusion.5), kind=kLoop, calls=%fused_computation.10.clone.1 | loop fusion | flops 12566528 | bytes 147456 | tf_op jit(solution)/shard_map/while/body/eval_jaxpr/reduce_sum | solution.py:63
  185.2 2.1 convolution_bitcast_fusion
  188.2 32.4 %all-reduce.6.cloned.1.call-done = f32[3,16384]{1,0:T(4,128)} async-done(((f32[3,16384]{1,0:T(4,128)}), f32[3,16384]{1,0:T(4,128)}) %all-reduce.6.cloned.1.call-update) | async-done | bytes 196624 | tf_op jit(solution)/shard_map/psum | solution.py:76
  (139 shorter events, 27.8 us)
Async XLA Ops:
  6.5 1.0 copy-start
  6.5 124.6 %all-reduce.4.cloned.1.call-start = ((), (), s32[]{:S(2)}) async-start(), calls=%async_computation | async-start | bytes 131072 | tf_op jit(solution)/shard_map/psum | solution.py:55
  9.4 1.7 copy-start.9
  9.4 1.7 copy-start.7
  13.6 0.8 copy-start.4
  15.4 40.8 %copy-start.1 = (s32[1,128]{1,0:T(1,128)S(1)}, s32[1,128]{1,0:T(1,128)}, u32[]{:S(2)}) copy-start(s32[1,128]{1,0:T(1,128)} %param.19) | copy-start | bytes 1540
  15.4 43.6 %copy-start.11 = (u32[32]{0:T(128)S(1)}, u32[32]{0:T(128)}, u32[]{:S(2)}) copy-start(u32[32]{0:T(128)} %constant.81) | copy-start | bytes 388
  15.4 45.0 %copy-start.10 = (f32[1,16]{1,0:T(1,128)S(1)}, f32[1,16]{1,0:T(1,128)}, u32[]{:S(2)}) copy-start(f32[1,16]{1,0:T(1,128)} %param.20) | copy-start | bytes 196
  15.5 68.2 %copy-start.8 = (f32[3,128]{1,0:T(4,128)S(1)}, f32[3,128]{1,0:T(4,128)}, u32[]{:S(2)}) copy-start(f32[3,128]{1,0:T(4,128)} %param.22) | copy-start | bytes 4612
  15.5 68.2 %copy-start.3 = (f32[3,128,128]{2,1,0:T(8,128)S(1)}, f32[3,128,128]{2,1,0:T(8,128)}, u32[]{:S(2)}) copy-start(f32[3,128,128]{2,1,0:T(8,128)} %param.21) | copy-start | bytes 589828
  59.0 161.5 %all-reduce.6.cloned.1.call-start = ((), (), s32[]{:S(2)}) async-start(), calls=%async_computation.1 | async-start | bytes 524288 | tf_op jit(solution)/shard_map/psum | solution.py:76
  131.1 5.7 %copy-start.2 = (f32[128,128]{1,0:T(8,128)S(1)}, f32[128,128]{1,0:T(8,128)}, u32[]{:S(2)}) copy-start(f32[128,128]{1,0:T(8,128)} %all-reduce.4.cloned.1.call-done) | copy-start | bytes 196612
  138.0 2.5 %copy-start.6 = (f32[3,128]{1,0:T(4,128)S(1)}, f32[3,128]{1,0:T(4,128)}, u32[]{:S(2)}) copy-start(f32[3,128]{1,0:T(4,128)} %param.23) | copy-start | bytes 4612
  141.2 44.0 %copy-start.5 = (s32[1,256]{1,0:T(1,128)S(1)}, s32[1,256]{1,0:T(1,128)}, u32[]{:S(2)}) copy-start(s32[1,256]{1,0:T(1,128)} %param.18) | copy-start | bytes 3076
Sparse Core Ops, SparseCore 0:
  59.1 71.9 all-reduce.3
  188.3 32.1 all-reduce.5
where the time goes:
time: 230 us; the launch traced here: 229 us
  other arithmetic  86.2 us (37%)
  waiting for transfers between devices  79.7 us (35%)
  blocking collectives  23.1 us (10%)
  between operations  14.5 us (6%)
  local copies, waits for them, and re-layouts  12.7 us (6%)
  matrix products  12.1 us (5%)
    psum x1, waiting for transfers between devices, per_device(): lax.psum(jnp.dot(halo_selection, pair_rows, precision=lax.Precision.HIGHE...  47.3 us
    reduce_sum x8, other arithmetic, project(): return jnp.sum(weight_part[:, :, None] * basis, axis=1)  39.8 us
    reduce_sum x8, other arithmetic, evaluate(): scalar = jnp.sum(basis * coef_part[:, None, :], axis=2)  37.7 us
    psum x1, waiting for transfers between devices, per_device(): return lax.psum(partial_halo_sum, 'halo')  32.4 us
    unnamed x1, blocking collectives  23.1 us
    dot_general x21, matrix products, relax(): mixed = jnp.dot(state[comp], mixing[comp], precision=lax.Precision.HIGHEST)  9.13 us
    dynamic_update_slice x8, other arithmetic, per_device(): shifted_positions = lax.map(evaluate, (offset_blocks, coef_rows))  5.63 us
  transfers between devices with their start and end apart: 2, of which 2 were waited for; matrix products, arithmetic and copies ran while one was open for 0% of the time, Pallas kernels for 0%

commit v1 on v0

--- a/solution.py
+++ b/solution.py
@@ -52,7 +52,12 @@
     slot_total = halo_slot.shape[1]
     wanted = jnp.arange(slot_total, dtype=jnp.int32)
     halo_selection = (slot_ids[None, :] == wanted[:, None]).astype(jnp.float32)
-    dense = lax.psum(jnp.dot(halo_selection, pair_rows, precision=lax.Precision.HIGHEST), "space")
+    dense = jnp.sum(
+        lax.all_gather(
+            jnp.dot(halo_selection, pair_rows, precision=lax.Precision.HIGHEST), "space"
+        ),
+        axis=0,
+    )
     all_feedback = lax.all_gather(feedback[0], "space", axis=0, tiled=True)
     coef_table = relax(jnp.log1p(dense), all_feedback, mixing, drive, readout)
     coef_rows = coef_table[slot_ids].reshape(-1, block, knots)

time: 230 us -> 208 us (0.904)
  waiting for transfers between devices: 79.7 us -> 29.7 us
  blocking collectives: 23.1 us -> 54.6 us
  local copies, waits for them, and re-layouts: 12.7 us -> 19 us
  matrix products: 12.1 us -> 6.83 us
  other arithmetic: 86.2 us -> 81.6 us
    psum x1 -> x0, waiting for transfers between devices: 47.3 us -> none  [per_device(): lax.psum(jnp.dot(halo_selection, pair_rows, precision=lax.Precision.HIGHE...]
    all_gather x0 -> x1, blocking collectives: none -> 33.1 us  [per_device(): lax.all_gather(jnp.dot(halo_selection, pair_rows, precision=lax.Precision...]
    mul x8, local copies, waits for them, and re-layouts: 0.08 us -> 5.8 us  [evaluate(): scalar = jnp.sum(basis * coef_part[:, None, :], axis=2)]
    dynamic_update_slice x8, other arithmetic: 5.63 us -> 0.21 us  [per_device(): shifted_positions = lax.map(evaluate, (offset_blocks, coef_rows))]
    dot_general x21, matrix products: 9.13 us -> 5.94 us  [relax(): mixed = jnp.dot(state[comp], mixing[comp], precision=lax.Precision.HIGHEST)]
    psum x1, waiting for transfers between devices: 32.4 us -> 29.7 us  [per_device(): return lax.psum(partial_halo_sum, 'halo')]
  transfers between devices with their start and end apart: 2 -> 1, of which waited for: 2 -> 1; matrix products, arithmetic and copies ran while one was open for 0% -> 0% of each run, Pallas kernels for 0% -> 0%
where the time goes in v1:
time: 208 us; the launch traced here: 207 us
  other arithmetic  81.6 us (39%)
  blocking collectives  54.6 us (26%)
  waiting for transfers between devices  29.7 us (14%)
  local copies, waits for them, and re-layouts  19 us (9%)
  between operations  14.4 us (7%)
  matrix products  6.83 us (3%)
    reduce_sum x8, other arithmetic, project(): return jnp.sum(weight_part[:, :, None] * basis, axis=1)  39.8 us
    reduce_sum x8, other arithmetic, evaluate(): scalar = jnp.sum(basis * coef_part[:, None, :], axis=2)  37.6 us
    all_gather x1, blocking collectives, per_device(): lax.all_gather(jnp.dot(halo_selection, pair_rows, precision=lax.Precision...  33.1 us
    psum x1, waiting for transfers between devices, per_device(): return lax.psum(partial_halo_sum, 'halo')  29.7 us
    unnamed x1, blocking collectives  21.5 us
    dot_general x21, matrix products, relax(): mixed = jnp.dot(state[comp], mixing[comp], precision=lax.Precision.HIGHEST)  5.94 us
    mul x8, local copies, waits for them, and re-layouts, evaluate(): scalar = jnp.sum(basis * coef_part[:, None, :], axis=2)  5.8 us
    unnamed x28, local copies, waits for them, and re-layouts  4.27 us
  transfers between devices with their start and end apart: 1, of which 1 were waited for; matrix products, arithmetic and copies ran while one was open for 0% of the time, Pallas kernels for 0%

profile of v1, /device:TPU:0, one launch (start us, length us, event | category | flops | bytes accessed | tf_op | source)
XLA Modules:
  0.0 206.8 jit_solution(8400934081237324058)
XLA Ops:
  7.5 1.9 gather_fusion
  15.4 40.7 %while.20 = (s32[]{:T(128)}, f32[8,32,128]{2,1,0:T(8,128)S(1)}, f32[8,32,512]{2,1,0:T(8,128)S(1)}, f32[8,3,32,512]{3,2,1,0:T(8,128)S(1)}, s32[]{:T(128)}) while((s32[]{:T(128)}, f32[8,32,128]{2,1,0:T(8,128)S(1)}, f32[8,32,512]{2,1,0:T(8,128)S(1)}, f32[8,3,32,512]{3,2,1,0:T(8,128)S(1)}, s32[]{:T(128)}) %tuple.48), condition=%wide.region_3.4_spmd, body=%wide.region_0.3_spmd.sunk | while | flops 12677122 | bytes 704585 | solution.py:51
  15.5 5.0 %multiply_reduce_fusion.9 = f32[32,128]{1,0:T(8,128)S(1)} fusion(f32[32,512]{1,0:T(8,128)S(1)} %sqrt_multiply_fusion.4, f32[32,512]{1,0:T(8,128)S(1)} %dynamic-slice_bitcast_fusion.4), kind=kLoop, calls=%fused_computation.5.clone.1 | loop fusion | flops 12578816 | bytes 147456 | tf_op jit(solution)/shard_map/while/body/eval_jaxpr/reduce_sum | solution.py:49
  20.6 5.0 %multiply_reduce_fusion.9 = f32[32,128]{1,0:T(8,128)S(1)} fusion(f32[32,512]{1,0:T(8,128)S(1)} %sqrt_multiply_fusion.4, f32[32,512]{1,0:T(8,128)S(1)} %dynamic-slice_bitcast_fusion.4), kind=kLoop, calls=%fused_computation.5.clone.1 | loop fusion | flops 12578816 | bytes 147456 | tf_op jit(solution)/shard_map/while/body/eval_jaxpr/reduce_sum | solution.py:49
  25.7 5.0 %multiply_reduce_fusion.9 = f32[32,128]{1,0:T(8,128)S(1)} fusion(f32[32,512]{1,0:T(8,128)S(1)} %sqrt_multiply_fusion.4, f32[32,512]{1,0:T(8,128)S(1)} %dynamic-slice_bitcast_fusion.4), kind=kLoop, calls=%fused_computation.5.clone.1 | loop fusion | flops 12578816 | bytes 147456 | tf_op jit(solution)/shard_map/while/body/eval_jaxpr/reduce_sum | solution.py:49
  30.8 5.0 %multiply_reduce_fusion.9 = f32[32,128]{1,0:T(8,128)S(1)} fusion(f32[32,512]{1,0:T(8,128)S(1)} %sqrt_multiply_fusion.4, f32[32,512]{1,0:T(8,128)S(1)} %dynamic-slice_bitcast_fusion.4), kind=kLoop, calls=%fused_computation.5.clone.1 | loop fusion | flops 12578816 | bytes 147456 | tf_op jit(solution)/shard_map/while/body/eval_jaxpr/reduce_sum | solution.py:49
  35.9 5.0 %multiply_reduce_fusion.9 = f32[32,128]{1,0:T(8,128)S(1)} fusion(f32[32,512]{1,0:T(8,128)S(1)} %sqrt_multiply_fusion.4, f32[32,512]{1,0:T(8,128)S(1)} %dynamic-slice_bitcast_fusion.4), kind=kLoop, calls=%fused_computation.5.clone.1 | loop fusion | flops 12578816 | bytes 147456 | tf_op jit(solution)/shard_map/while/body/eval_jaxpr/reduce_sum | solution.py:49
  41.0 5.0 %multiply_reduce_fusion.9 = f32[32,128]{1,0:T(8,128)S(1)} fusion(f32[32,512]{1,0:T(8,128)S(1)} %sqrt_multiply_fusion.4, f32[32,512]{1,0:T(8,128)S(1)} %dynamic-slice_bitcast_fusion.4), kind=kLoop, calls=%fused_computation.5.clone.1 | loop fusion | flops 12578816 | bytes 147456 | tf_op jit(solution)/shard_map/while/body/eval_jaxpr/reduce_sum | solution.py:49
  46.1 5.0 %multiply_reduce_fusion.9 = f32[32,128]{1,0:T(8,128)S(1)} fusion(f32[32,512]{1,0:T(8,128)S(1)} %sqrt_multiply_fusion.4, f32[32,512]{1,0:T(8,128)S(1)} %dynamic-slice_bitcast_fusion.4), kind=kLoop, calls=%fused_computation.5.clone.1 | loop fusion | flops 12578816 | bytes 147456 | tf_op jit(solution)/shard_map/while/body/eval_jaxpr/reduce_sum | solution.py:49
  51.2 5.0 %multiply_reduce_fusion.9 = f32[32,128]{1,0:T(8,128)S(1)} fusion(f32[32,512]{1,0:T(8,128)S(1)} %sqrt_multiply_fusion.4, f32[32,512]{1,0:T(8,128)S(1)} %dynamic-slice_bitcast_fusion.4), kind=kLoop, calls=%fused_computation.5.clone.1 | loop fusion | flops 12578816 | bytes 147456 | tf_op jit(solution)/shard_map/while/body/eval_jaxpr/reduce_sum | solution.py:49
  56.2 1.9 gather_fusion.2
  58.3 33.1 %all-gather = f32[1024,128]{1,0:T(8,128)S(1)} all-gather(f32[128,128]{1,0:T(8,128)S(1)} %fusion.67), channel_id=2, replica_groups=mesh['space'=8,'halo'=4] {'space'}, dimensions={0}, use_global_device_ids=true | all-gather | bytes 589824 | tf_op jit(solution)/shard_map/all_gather | solution.py:56
  92.8 21.5 %all-reduce = f32[128]{0:T(128)S(1)} all-reduce(f32[128]{0:T(128)S(1)} %bitcast_dynamic-update-slice_fusion.2), channel_id=3, replica_groups=mesh['space'=8,'halo'=4] {'space'}, use_global_device_ids=true, to_apply=%add | all-reduce | flops 128 | bytes 1024
  122.7 44.3 %while.21 = (s32[]{:T(128)}, f32[8,3,32,512]{3,2,0,1:T(8,128)S(1)}, f32[8,3,32,512]{3,2,1,0:T(8,128)S(1)}, f32[8,32,128]{2,1,0:T(8,128)}, s32[]{:T(128)}) while((s32[]{:T(128)}, f32[8,3,32,512]{3,2,0,1:T(8,128)S(1)}, f32[8,3,32,512]{3,2,1,0:T(8,128)S(1)}, f32[8,32,128]{2,1,0:T(8,128)}, s32[]{:T(128)}) %tuple.49), condition=%wide.region_12.13_spmd, body=%wide.region_9.12_spmd.sunk | while | flops 12713986 | bytes 1032265 | solution.py:71
  123.5 4.7 %multiply_reduce_fusion.11 = f32[32,512]{1,0:T(8,128)S(1)} fusion(f32[32,128]{1,0:T(8,128)S(1)} %dynamic-slice_bitcast_fusion.5, f32[32,512]{1,0:T(8,128)S(1)} %sqrt_multiply_fusion.5), kind=kLoop, calls=%fused_computation.10.clone.1 | loop fusion | flops 12566528 | bytes 147456 | tf_op jit(solution)/shard_map/while/body/eval_jaxpr/reduce_sum | solution.py:68
  129.0 4.7 %multiply_reduce_fusion.11 = f32[32,512]{1,0:T(8,128)S(1)} fusion(f32[32,128]{1,0:T(8,128)S(1)} %dynamic-slice_bitcast_fusion.5, f32[32,512]{1,0:T(8,128)S(1)} %sqrt_multiply_fusion.5), kind=kLoop, calls=%fused_computation.10.clone.1 | loop fusion | flops 12566528 | bytes 147456 | tf_op jit(solution)/shard_map/while/body/eval_jaxpr/reduce_sum | solution.py:68
  134.6 4.7 %multiply_reduce_fusion.11 = f32[32,512]{1,0:T(8,128)S(1)} fusion(f32[32,128]{1,0:T(8,128)S(1)} %dynamic-slice_bitcast_fusion.5, f32[32,512]{1,0:T(8,128)S(1)} %sqrt_multiply_fusion.5), kind=kLoop, calls=%fused_computation.10.clone.1 | loop fusion | flops 12566528 | bytes 147456 | tf_op jit(solution)/shard_map/while/body/eval_jaxpr/reduce_sum | solution.py:68
  140.1 4.7 %multiply_reduce_fusion.11 = f32[32,512]{1,0:T(8,128)S(1)} fusion(f32[32,128]{1,0:T(8,128)S(1)} %dynamic-slice_bitcast_fusion.5, f32[32,512]{1,0:T(8,128)S(1)} %sqrt_multiply_fusion.5), kind=kLoop, calls=%fused_computation.10.clone.1 | loop fusion | flops 12566528 | bytes 147456 | tf_op jit(solution)/shard_map/while/body/eval_jaxpr/reduce_sum | solution.py:68
  145.7 4.7 %multiply_reduce_fusion.11 = f32[32,512]{1,0:T(8,128)S(1)} fusion(f32[32,128]{1,0:T(8,128)S(1)} %dynamic-slice_bitcast_fusion.5, f32[32,512]{1,0:T(8,128)S(1)} %sqrt_multiply_fusion.5), kind=kLoop, calls=%fused_computation.10.clone.1 | loop fusion | flops 12566528 | bytes 147456 | tf_op jit(solution)/shard_map/while/body/eval_jaxpr/reduce_sum | solution.py:68
  151.2 4.7 %multiply_reduce_fusion.11 = f32[32,512]{1,0:T(8,128)S(1)} fusion(f32[32,128]{1,0:T(8,128)S(1)} %dynamic-slice_bitcast_fusion.5, f32[32,512]{1,0:T(8,128)S(1)} %sqrt_multiply_fusion.5), kind=kLoop, calls=%fused_computation.10.clone.1 | loop fusion | flops 12566528 | bytes 147456 | tf_op jit(solution)/shard_map/while/body/eval_jaxpr/reduce_sum | solution.py:68
  156.8 4.7 %multiply_reduce_fusion.11 = f32[32,512]{1,0:T(8,128)S(1)} fusion(f32[32,128]{1,0:T(8,128)S(1)} %dynamic-slice_bitcast_fusion.5, f32[32,512]{1,0:T(8,128)S(1)} %sqrt_multiply_fusion.5), kind=kLoop, calls=%fused_computation.10.clone.1 | loop fusion | flops 12566528 | bytes 147456 | tf_op jit(solution)/shard_map/while/body/eval_jaxpr/reduce_sum | solution.py:68
  162.3 4.7 %multiply_reduce_fusion.11 = f32[32,512]{1,0:T(8,128)S(1)} fusion(f32[32,128]{1,0:T(8,128)S(1)} %dynamic-slice_bitcast_fusion.5, f32[32,512]{1,0:T(8,128)S(1)} %sqrt_multiply_fusion.5), kind=kLoop, calls=%fused_computation.10.clone.1 | loop fusion | flops 12566528 | bytes 147456 | tf_op jit(solution)/shard_map/while/body/eval_jaxpr/reduce_sum | solution.py:68
  168.6 29.7 %all-reduce.3.cloned.1.call-done = f32[3,16384]{1,0:T(4,128)} async-done(((f32[3,16384]{1,0:T(4,128)}), f32[3,16384]{1,0:T(4,128)}) %all-reduce.3.cloned.1.call-update) | async-done | bytes 196624 | tf_op jit(solution)/shard_map/psum | solution.py:81
  198.3 1.7 copy.51
  (136 shorter events, 24.7 us)
Async XLA Ops:
  6.5 1.0 copy-start
  6.5 191.8 %all-reduce.3.cloned.1.call-start = ((), (), s32[]{:S(2)}) async-start(), calls=%async_computation | async-start | bytes 524288 | tf_op jit(solution)/shard_map/psum | solution.py:81
  9.4 1.7 copy-start.8
  9.4 1.7 copy-start.6
  13.6 0.8 copy-start.3
  15.4 40.8 %copy-start.1 = (s32[1,128]{1,0:T(1,128)S(1)}, s32[1,128]{1,0:T(1,128)}, u32[]{:S(2)}) copy-start(s32[1,128]{1,0:T(1,128)} %param.19) | copy-start | bytes 1540
  56.2 35.3 %copy-start.10 = (u32[32]{0:T(128)S(1)}, u32[32]{0:T(128)}, u32[]{:S(2)}) copy-start(u32[32]{0:T(128)} %constant.81) | copy-start | bytes 388
  56.2 36.5 %copy-start.9 = (f32[1,16]{1,0:T(1,128)S(1)}, f32[1,16]{1,0:T(1,128)}, u32[]{:S(2)}) copy-start(f32[1,16]{1,0:T(1,128)} %param.20) | copy-start | bytes 196
  56.2 58.1 %copy-start.7 = (f32[3,128]{1,0:T(4,128)S(1)}, f32[3,128]{1,0:T(4,128)}, u32[]{:S(2)}) copy-start(f32[3,128]{1,0:T(4,128)} %param.22) | copy-start | bytes 4612
  56.2 58.1 %copy-start.2 = (f32[3,128,128]{2,1,0:T(8,128)S(1)}, f32[3,128,128]{2,1,0:T(8,128)}, u32[]{:S(2)}) copy-start(f32[3,128,128]{2,1,0:T(8,128)} %param.21) | copy-start | bytes 589828
  116.8 3.7 %copy-start.5 = (f32[3,128]{1,0:T(4,128)S(1)}, f32[3,128]{1,0:T(4,128)}, u32[]{:S(2)}) copy-start(f32[3,128]{1,0:T(4,128)} %param.23) | copy-start | bytes 4612
  122.7 44.3 %copy-start.4 = (s32[1,256]{1,0:T(1,128)S(1)}, s32[1,256]{1,0:T(1,128)}, u32[]{:S(2)}) copy-start(s32[1,256]{1,0:T(1,128)} %param.18) | copy-start | bytes 3076
Sparse Core Ops, SparseCore 0:
  168.7 29.5 all-reduce.2
